TPU v7x, 32 devices: a whole 2x2x4 slice. The times are simulated.
32 devices in a mesh: dp: 8 (over y, x, core), mp: 4 (over z).
Axes of the slice: x: 2, y: 2, z: 4, core: 2. Of those that a mesh axis runs over, the one named last changes fastest.
Arguments:
- hidden: bfloat16 [24576, 768], P('dp'), may hold values from -6 to 6
- timesteps: int32 [144], P('dp'), may hold values from 0 to 999
- cotangent: bfloat16 [24576, 768], P('dp'), may hold values from -6 to 6
- time_table: bfloat16 [1000, 768], replicated, may hold values from -3 to 3
- first_gain: float32 [768], replicated, may hold values from 0.25 to 1.75
- first_shift: float32 [768], replicated, may hold values from -1.5 to 1.5
- qkv_weight: bfloat16 [3, 768, 768], P(None, None, 'mp'), may hold values from -0.21875 to 0.21875
- out_weight: bfloat16 [768, 768], P('mp'), may hold values from -0.875 to 0.875
- out_bias: float32 [768], replicated, may hold values from -1.5 to 1.5
- second_gain: float32 [768], replicated, may hold values from 0.25 to 1.75
- second_shift: float32 [768], replicated, may hold values from -1.5 to 1.5
- up_weight: bfloat16 [768, 3072], P(None, 'mp'), may hold values from -0.21875 to 0.21875
- up_bias: float32 [3072], P('mp'), may hold values from -2.5 to 2.5
- down_weight: bfloat16 [3072, 768], P('mp'), may hold values from -0.15625 to 0.15625
- down_bias: float32 [768], replicated, may hold values from -1.5 to 1.5
Outputs:
- output: bfloat16 [24576, 768], P('dp')
- grad_hidden: bfloat16 [24576, 768], P('dp')
- grad_table: float32 [1000, 768], P(None, 'mp')
- grad_first_gain: float32 [768], replicated
- grad_first_shift: float32 [768], replicated
- grad_qkv_weight: float32 [3, 768, 768], P(None, 'dp', 'mp')
- grad_out_weight: float32 [768, 768], P('mp', 'dp')
- grad_out_bias: float32 [768], replicated
- grad_second_gain: float32 [768], replicated
- grad_second_shift: float32 [768], replicated
- grad_up_weight: float32 [768, 3072], P('dp', 'mp')
- grad_up_bias: float32 [3072], P('mp')
- grad_down_weight: float32 [3072, 768], P('mp', 'dp')
- grad_down_bias: float32 [768], replicated
All inputs are finite; a program needn't handle non-finite values.
Results may differ from a plain program's by a relative error of at most 0.02.
Values may be sent and summed in bfloat16 or wider, within the bound.
A program may use at most 192 MiB of HBM per device.

v0:
```python
from functools import partial
import jax
import jax.numpy as jnp
from jax import lax
from jax.sharding import PartitionSpec as P

HD = 64
LEN_A = 128
LEN_B = 256
BLOCK = 512


def layer_norm(rows_in, gain_vec, shift_vec):
    centre = jnp.mean(rows_in, axis=-1, keepdims=True)
    offset = rows_in - centre
    spread = jnp.mean(offset * offset, axis=-1, keepdims=True)
    return offset * lax.rsqrt(spread + 1e-05) * gain_vec + shift_vec


def block_scores(queries, key_rows, seg_len):
    scores = jnp.einsum(
        "qhd,khd->hqk", queries, key_rows, preferred_element_type=jnp.float32
    ) * HD ** (-0.5)
    segment = lax.broadcasted_iota(jnp.int32, (BLOCK,), 0) // seg_len
    same_row = segment[:, None] == segment[None, :]
    return jnp.where(same_row[None], scores, -1000000000.0)


def attend_block(queries, key_rows, value_rows, seg_len):
    scores = block_scores(queries, key_rows, seg_len)
    log_total = jax.nn.logsumexp(scores, axis=-1)
    attn_probs = jnp.exp(scores - log_total[..., None]).astype(jnp.bfloat16)
    context = jnp.einsum("hqk,khd->qhd", attn_probs, value_rows, preferred_element_type=jnp.float32)
    return (context, log_total)


def attend_pair(pieces):
    queries, key_rows, value_rows = pieces
    lead_out, lead_log = attend_block(queries[0], key_rows[0], value_rows[0], LEN_A)
    tail_out, tail_log = attend_block(queries[1], key_rows[1], value_rows[1], LEN_B)
    return (jnp.stack([lead_out, tail_out]), jnp.stack([lead_log, tail_log]))


def attend_back_block(queries, key_rows, value_rows, grad_out, log_total, seg_len):
    scores = block_scores(queries, key_rows, seg_len)
    attn_probs = jnp.exp(scores - log_total[..., None])
    grad_probs = jnp.einsum(
        "qhd,khd->hqk", grad_out, value_rows, preferred_element_type=jnp.float32
    )
    grad_values = jnp.einsum(
        "hqk,qhd->khd",
        attn_probs.astype(jnp.bfloat16),
        grad_out,
        preferred_element_type=jnp.float32,
    )
    inner_sum = jnp.sum(attn_probs * grad_probs, axis=-1, keepdims=True)
    grad_scores = (attn_probs * (grad_probs - inner_sum)).astype(jnp.bfloat16)
    scale = HD ** (-0.5)
    grad_queries = (
        jnp.einsum("hqk,khd->qhd", grad_scores, key_rows, preferred_element_type=jnp.float32)
        * scale
    )
    grad_keys = (
        jnp.einsum("hqk,qhd->khd", grad_scores, queries, preferred_element_type=jnp.float32) * scale
    )
    return (grad_queries, grad_keys, grad_values)


def attend_back_pair(pieces):
    queries, key_rows, value_rows, grad_out, log_total = pieces
    lead = attend_back_block(
        queries[0], key_rows[0], value_rows[0], grad_out[0], log_total[0], LEN_A
    )
    tail = attend_back_block(
        queries[1], key_rows[1], value_rows[1], grad_out[1], log_total[1], LEN_B
    )
    return tuple((jnp.stack([lead[index], tail[index]]) for index in range(3)))


def local(
    hidden,
    timesteps,
    cotangent,
    time_table,
    first_gain,
    first_shift,
    qkv_weight,
    out_weight,
    out_bias,
    second_gain,
    second_shift,
    up_weight,
    up_bias,
    down_weight,
    down_bias,
):
    count = hidden.shape[0]
    width = hidden.shape[1]
    local_width = qkv_weight.shape[2]
    local_heads = local_width // HD
    pairs_dev = count // (2 * BLOCK)
    row_count = timesteps.shape[0]
    members = lax.axis_size("mp")
    row_emb = (
        jnp.take(time_table, timesteps, axis=0).astype(jnp.float32).reshape(pairs_dev, 6, width)
    )
    lead_emb = jnp.broadcast_to(row_emb[:, :4, None, :], (pairs_dev, 4, LEN_A, width)).reshape(
        pairs_dev, BLOCK, width
    )
    tail_emb = jnp.broadcast_to(row_emb[:, 4:, None, :], (pairs_dev, 2, LEN_B, width)).reshape(
        pairs_dev, BLOCK, width
    )
    stream_in = jnp.concatenate([lead_emb, tail_emb], axis=1).reshape(count, width) + hidden.astype(
        jnp.float32
    )

    def front(stream_rows):
        normed = layer_norm(stream_rows, first_gain, first_shift).astype(jnp.bfloat16)
        proj = jnp.einsum(
            "td,cde->cte", normed, qkv_weight, preferred_element_type=jnp.float32
        ).astype(jnp.bfloat16)
        shaped = proj.reshape(3, pairs_dev, 2, BLOCK, local_heads, HD)
        context, log_total = lax.map(attend_pair, (shaped[0], shaped[1], shaped[2]))
        return (normed, shaped, context.reshape(count, local_width).astype(jnp.bfloat16), log_total)

    def mlp_front(normed_rows):
        pre_act = jnp.dot(normed_rows, up_weight, preferred_element_type=jnp.float32) + up_bias
        return (pre_act, jax.nn.gelu(pre_act, approximate=True).astype(jnp.bfloat16))

    normed, shaped, context, log_total = front(stream_in)
    attn_part = jnp.dot(context, out_weight, preferred_element_type=jnp.float32)
    attn_total = lax.psum(attn_part.astype(jnp.bfloat16), "mp").astype(jnp.float32)
    middle = stream_in + attn_total + out_bias
    normed_two = layer_norm(middle, second_gain, second_shift).astype(jnp.bfloat16)
    pre_act, activated = mlp_front(normed_two)
    mlp_part = jnp.dot(activated, down_weight, preferred_element_type=jnp.float32)
    result = middle + lax.psum(mlp_part.astype(jnp.bfloat16), "mp").astype(jnp.float32) + down_bias
    grad_top = cotangent.astype(jnp.float32)
    pre_act, activated = mlp_front(lax.optimization_barrier(normed_two))
    grad_down = jnp.einsum("tf,td->fd", activated, cotangent, preferred_element_type=jnp.float32)
    grad_down_bias = jnp.sum(grad_top, axis=0)
    grad_act = jnp.einsum("td,fd->tf", cotangent, down_weight, preferred_element_type=jnp.float32)
    slope_pull = jax.vjp(partial(jax.nn.gelu, approximate=True), pre_act)[1]
    grad_pre = slope_pull(grad_act)[0].astype(jnp.bfloat16)
    grad_up = jnp.einsum("td,tf->df", normed_two, grad_pre, preferred_element_type=jnp.float32)
    grad_up_bias = jnp.sum(grad_pre, axis=0, dtype=jnp.float32)
    norm_part = jnp.einsum("tf,df->td", grad_pre, up_weight, preferred_element_type=jnp.float32)
    norm_grad = lax.psum(norm_part.astype(jnp.bfloat16), "mp").astype(jnp.float32)
    second_pull = jax.vjp(layer_norm, middle, second_gain, second_shift)[1]
    grad_mid, grad_gain_two, grad_shift_two = second_pull(norm_grad)
    grad_mid = grad_mid + grad_top
    grad_mid_low = grad_mid.astype(jnp.bfloat16)
    grad_out_bias = jnp.sum(grad_mid, axis=0)
    normed, shaped, context, log_total = front(lax.optimization_barrier(stream_in))
    grad_out_w = jnp.einsum("te,td->ed", context, grad_mid_low, preferred_element_type=jnp.float32)
    grad_context = jnp.einsum(
        "td,ed->te", grad_mid_low, out_weight, preferred_element_type=jnp.float32
    ).astype(jnp.bfloat16)
    grad_context = grad_context.reshape(pairs_dev, 2, BLOCK, local_heads, HD)
    grad_query, grad_key, grad_value = lax.map(
        attend_back_pair, (shaped[0], shaped[1], shaped[2], grad_context, log_total)
    )
    grad_proj = (
        jnp.stack([grad_query, grad_key, grad_value])
        .reshape(3, count, local_width)
        .astype(jnp.bfloat16)
    )
    grad_qkv = jnp.einsum("td,cte->cde", normed, grad_proj, preferred_element_type=jnp.float32)
    first_part = jnp.einsum(
        "cte,cde->td", grad_proj, qkv_weight, preferred_element_type=jnp.float32
    )
    first_grad = lax.psum(first_part.astype(jnp.bfloat16), "mp").astype(jnp.float32)
    first_pull = jax.vjp(layer_norm, stream_in, first_gain, first_shift)[1]
    grad_in, grad_gain_one, grad_shift_one = first_pull(first_grad)
    grad_in = grad_in + grad_mid
    output = result.astype(jnp.bfloat16)
    columns = width // members
    own_cols = lax.dynamic_slice_in_dim(
        grad_in, lax.axis_index("mp") * columns, columns, 1
    ).reshape(pairs_dev, 2 * BLOCK, columns)
    lead_rows = jnp.sum(own_cols[:, :BLOCK].reshape(pairs_dev, 4, LEN_A, columns), axis=2)
    tail_rows = jnp.sum(own_cols[:, BLOCK:].reshape(pairs_dev, 2, LEN_B, columns), axis=2)
    row_grad = jnp.concatenate([lead_rows, tail_rows], axis=1).reshape(row_count, columns)
    chosen = (
        timesteps[:, None] == lax.broadcasted_iota(jnp.int32, (1, time_table.shape[0]), 1)
    ).astype(jnp.float32)
    table_grad = jnp.dot(
        chosen.T, row_grad, precision=lax.Precision.HIGHEST, preferred_element_type=jnp.float32
    )
    grad_qkv, grad_out_w, grad_up, grad_down = (
        lax.psum_scatter(grad_qkv, "dp", scatter_dimension=1, tiled=True),
        lax.psum_scatter(grad_out_w, "dp", scatter_dimension=1, tiled=True),
        lax.psum_scatter(grad_up, "dp", scatter_dimension=0, tiled=True),
        lax.psum_scatter(grad_down, "dp", scatter_dimension=1, tiled=True),
    )
    (
        table_grad,
        grad_gain_one,
        grad_shift_one,
        grad_out_bias,
        grad_gain_two,
        grad_shift_two,
        grad_up_bias,
        grad_down_bias,
    ) = lax.psum(
        (
            table_grad,
            grad_gain_one,
            grad_shift_one,
            grad_out_bias,
            grad_gain_two,
            grad_shift_two,
            grad_up_bias,
            grad_down_bias,
        ),
        "dp",
    )
    return (
        output,
        grad_in.astype(jnp.bfloat16),
        table_grad,
        grad_gain_one,
        grad_shift_one,
        grad_qkv,
        grad_out_w,
        grad_out_bias,
        grad_gain_two,
        grad_shift_two,
        grad_up,
        grad_up_bias,
        grad_down,
        grad_down_bias,
    )


def solution(mesh):
    return jax.shard_map(
        local,
        mesh=mesh,
        in_specs=(
            P("dp", None),
            P("dp"),
            P("dp", None),
            P(),
            P(),
            P(),
            P(None, None, "mp"),
            P("mp", None),
            P(),
            P(),
            P(),
            P(None, "mp"),
            P("mp"),
            P("mp", None),
            P(),
        ),
        out_specs=(
            P("dp", None),
            P("dp", None),
            P(None, "mp"),
            P(),
            P(),
            P(None, "dp", "mp"),
            P("mp", "dp"),
            P(),
            P(),
            P(),
            P("dp", "mp"),
            P("mp"),
            P("mp", "dp"),
            P(),
        ),
        check_vma=False,
    )
```

profile of v0, /device:TPU:0, one launch (start us, length us, event | category | flops | bytes accessed | tf_op | source)
XLA Modules:
  0.0 1124.5 jit_solution(4650453596753585933)
XLA Ops:
  12.4 6.6 pad_maximum_fusion
  19.0 9.7 fusion.139
  28.8 4.9 multiply_reduce_fusion.4
  35.1 3.5 fusion.104
  40.8 3.5 squeeze.178
  44.3 4.0 squeeze.177
  51.1 31.3 %while.45 = (s32[]{:T(128)}, bf16[3,2,512,3,64]{2,4,3,1,0:T(8,128)(2,1)}, bf16[3,2,512,3,64]{2,1,0,4,3:T(2,128)(2,1)}, bf16[3,2,512,3,64]{2,1,0,4,3:T(2,128)(2,1...) while((s32[]{:T(128)}, bf16[3,2,512,3,64]{2,4,3,1,0:T(8,128)(2,1)}, ...), condition=%wide.region_7.8_spmd, body=%wide.region_2.7_spmd.sunk | while | flops 421284864 | bytes 25809020 | solution.py:123
  86.3 3.6 convolution_convert_fusion.2
  90.1 4.2 reduce_sum.301
  94.2 4.8 multiply_reduce_fusion.2
  99.1 5.1 add_convert_fusion
  108.9 4.0 squeeze.181
  121.9 143.0 %all-reduce.7.cloned.1.call-done = bf16[3072,768]{1,0:T(8,128)(2,1)} async-done(((bf16[3072,768]{1,0:T(8,128)(2,1)}), bf16[3072,768]{1,0:T(8,128)(2,1)}) %all-reduce.7.cloned.1.call-update) | async-done | bytes 4718608 | tf_op jit(solution)/shard_map/psum | solution.py:132
  264.8 10.0 fusion.138
  274.9 4.9 multiply_reduce_fusion.3
  283.0 6.3 fusion.143
  289.4 12.0 %convert_reduce_fusion.3 = (f32[768]{0:T(1024)}, bf16[3072,768]{1,0:T(8,128)(2,1)S(1)}) fusion(f32[3072,768]{1,0:T(8,128)} %fusion.143, f32[768]{0:T(1024)S(1)} %copy-done.37, bf16[3072,768]{1,0:T(8,128)(2,1)S(1)} %bitcast.369, bf16[768,768]{1,0:T(8,128)(2,1)S(1)} %copy-done.33), kind=kOutput, calls=%fused_computation.213 | convolution fusion | flops 3678141696 | bytes 20060160 | tf_op jit(solution)/shard_map/td,fd->tf/dot_general | solution.py:142
  303.6 5.5 convolution_convert_fusion
  310.3 24.6 %while.46 = (s32[]{:T(128)}, bf16[3,2,512,3,64]{2,4,3,1,0:T(8,128)(2,1)}, f32[3,2,3,512]{3,2,1,0:T(4,128)S(1)}, bf16[3,2,512,3,64]{2,4,3,1,0:T(8,128)(2,1)}, bf1...) while((s32[]{:T(128)}, ...), condition=%wide.region_22.23_spmd, body=%wide.region_17.22_spmd.sunk | while | flops 421300224 | bytes 23522436 | solution.py:123
  334.9 3.5 copy.103
  338.4 3.9 convert_element_type.176
  342.3 137.8 %all-reduce.9.cloned.1.call-done = bf16[3072,768]{1,0:T(8,128)(2,1)} async-done(((bf16[3072,768]{1,0:T(8,128)(2,1)}), bf16[3072,768]{1,0:T(8,128)(2,1)}) %all-reduce.9.cloned.1.call-update) | async-done | bytes 4718608 | tf_op jit(solution)/shard_map/psum | solution.py:148
  480.2 8.4 convert_reduce_fusion.1
  488.6 8.3 fusion.102
  497.0 5.4 fusion.136
  502.4 3.3 convolution_convert_fusion.3
  509.5 4.4 reshape.677
  517.3 43.6 %while.47 = (s32[]{:T(128)}, bf16[3,2,512,3,64]{2,4,3,1,0:T(8,128)(2,1)}, bf16[3,2,512,3,64]{2,4,3,1,0:T(8,128)(2,1)}, bf16[3,2,512,3,64]{2,4,3,1,0:T(8,128)(2,1...) while((s32[]{:T(128)}, ...), condition=%wide.region_26.27_spmd, body=%wide.region_23.26_spmd.sunk | while | flops 1024463872 | bytes 55389380 | solution.py:160
  561.0 3.5 copy.102
  564.5 3.6 stack.128
  568.0 3.5 copy.100
  571.6 3.9 stack.126
  577.8 3.3 stack.127
  584.4 5.2 fusion.115
  592.3 4.8 reshape.697
  597.3 12.6 %convolution_convert_fusion.1 = bf16[3072,768]{1,0:T(8,128)(2,1)} fusion(bf16[768,768]{1,0:T(8,128)(2,1)S(1)} %copy-done.34, bf16[3072,768]{1,0:T(8,128)(2,1)} %copy-done.7, bf16[768,768]{1,0:T(8,128)(2,1)S(1)} %copy-done.32, f32[768]{0:T(1024)S(1)} %copy-done.38), kind=kOutput, calls=%fused_computation.224 | convolution fusion | flops 7273709568 | bytes 11799552 | tf_op jit(solution)/shard_map/dot_general | solution.py:136
  609.8 8.2 bitcast_convert_fusion
  618.1 9.1 fusion.144
  627.6 11.5 %fusion.111 = f32[768,768]{0,1:T(8,128)} fusion(bf16[3072,768]{1,0:T(8,128)(2,1)} %param.23, f32[3072,768]{1,0:T(8,128)} %fusion.143, f32[768]{0:T(1024)S(1)} %copy-done.38), kind=kOutput, calls=%fused_computation.233 | convolution fusion | flops 3647471616 | bytes 16518144 | tf_op jit(solution)/shard_map/tf,td->fd/dot_general | solution.py:140
  642.8 321.4 %all-reduce.13.cloned.1.call-done = (bf16[3072,768]{1,0:T(8,128)(2,1)}, bf16[3072,768]{1,0:T(8,128)(2,1)}) async-done(((bf16[3072,768]{1,0:T(8,128)(2,1)}, bf16[3072,768]{1,0:T(8,128)(2,1)}), (bf16[3072,768]{1,0:T(8,128)(2,1)}, bf16[3072,768]{1,0:T(8,128)(2,1)})) %all-reduce.13.cloned.1.call-update) | async-done | bytes 9437200 | tf_op jit(solution)/shard_map/psum | solution.py:137
  964.2 8.4 convert_reduce_fusion
  972.7 10.3 fusion.103
  983.2 6.6 fusion.137
  989.8 3.2 constant_dynamic-slice_fusion.8
  994.8 8.6 add_convert_fusion.1
  1003.5 24.4 %all-reduce = (f32[768]{0:T(1024)}, f32[768]{0:T(1024)}, f32[768]{0:T(1024)}, f32[768]{0:T(1024)}, f32[768]{0:T(1024)}, /*index=5*/f32[768]{0:T(1024)}, f32[768]{0:T(1024)}) all-reduce(f32[768]{0:T(1024)S(1)} %get-tuple-element.458, f32[768]{0:T(1024)S(1)} %get-tuple-element.462, ...), channel_id=1, replica_groups=mesh['dp'=8,'mp'=4] {'dp'}, use_global_device_ids=true, to_apply=%region_34.35 | all-reduce | flops 5376 | bytes 43008 | tf_op jit(solution)/shard_map/psum | solution.py:205
  1027.9 27.8 %reduce-scatter.11.cloned.1.call-done = f32[768,96]{0,1:T(8,128)} async-done(((f32[768,768]{0,1:T(8,128)}), f32[768,96]{0,1:T(8,128)}) %reduce-scatter.11.cloned.1.call-update) | async-done | bytes 294928 | tf_op jit(solution)/shard_map/reduce_scatter | solution.py:194
  1055.7 59.4 %all-reduce.11.cloned.1.call-done = f32[1000,192]{0,1:T(8,128)} async-done(((f32[1000,192]{0,1:T(8,128)}), f32[1000,192]{0,1:T(8,128)}) %all-reduce.11.cloned.1.call-update) | async-done | bytes 768016 | tf_op jit(solution)/shard_map/psum | solution.py:205
  (350 shorter events, 157.9 us)
Async XLA Ops:
  7.2 257.6 %all-reduce.7.cloned.1.call-start = ((), (), s32[]{:S(2)}) async-start(), calls=%async_computation.4 | async-start | bytes 9437184 | tf_op jit(solution)/shard_map/psum | solution.py:132
  19.0 14.8 %copy-start.35 = (bf16[3,768,192]{1,2,0:T(8,128)(2,1)S(1)}, bf16[3,768,192]{1,2,0:T(8,128)(2,1)}, u32[]{:S(2)}) copy-start(bf16[3,768,192]{1,2,0:T(8,128)(2,1)} %param.27) | copy-start | bytes 2654212
  28.7 5.0 copy-start.12
  28.7 6.4 copy-start.2
  28.8 6.4 copy-start.19
  28.8 6.4 copy-start.25
  90.0 390.2 %all-reduce.9.cloned.1.call-start = ((), (), s32[]{:S(2)}) async-start(), calls=%async_computation.5 | async-start | bytes 9437184 | tf_op jit(solution)/shard_map/psum | solution.py:148
  99.1 5.1 copy-start.36
  117.2 147.7 %copy-start.26 = (f32[768]{0:T(1024)S(1)}, f32[768]{0:T(1024)}, u32[]{:S(2)}) copy-start(f32[768]{0:T(1024)} %param.29) | copy-start | bytes 9220
  274.8 6.4 copy-start.3
  274.9 6.4 copy-start.18
  274.9 6.4 copy-start.27
  281.2 8.1 slice-start.11
  282.9 6.4 copy-start.7
  283.0 6.4 slice-start.12
  283.0 6.4 copy-start.33
  283.0 6.4 copy-start.37
  309.1 330.2 %reduce-scatter.15.cloned.1.call-start = ((), (), s32[]{:S(2)}) async-start(), calls=%async_computation.10 | async-start | bytes 884736
  480.2 8.4 copy-start.5
  480.2 16.8 %slice-start.3 = ((s8[9437184]{0:T(1024)(128)(4,1)}), s8[4194304]{0:T(1024)(128)(4,1)S(1)}, s32[]{:S(2)}) async-start(s8[9437184]{0:T(1024)(128)(4,1)} %bitcast.355), calls=%async_computation.15 | async-start | bytes 8388608
  480.2 16.8 %slice-start.4 = ((s8[9437184]{0:T(1024)(128)(4,1)}), s8[4194304]{0:T(1024)(128)(4,1)S(1)}, s32[]{:S(2)}) async-start(s8[9437184]{0:T(1024)(128)(4,1)} %bitcast.355), calls=%async_computation.16 | async-start | bytes 8388608
  480.2 16.8 %slice-start.13 = ((s8[4718592]{0:T(1024)(128)(4,1)}), s8[4194304]{0:T(1024)(128)(4,1)S(1)}, s32[]{:S(2)}) async-start(s8[4718592]{0:T(1024)(128)(4,1)} %bitcast.370), calls=%async_computation.25 | async-start | bytes 8388608
  488.6 8.4 slice-start.5
  488.6 8.4 slice-start.14
  509.4 131.4 %reduce-scatter.13.cloned.1.call-start = ((), (), s32[]{:S(2)}) async-start(), calls=%async_computation.9 | async-start | bytes 2211840
  564.5 11.0 copy-start.8
  597.2 367.0 %all-reduce.13.cloned.1.call-start = ((), (), s32[]{:S(2)}) async-start(), calls=%async_computation.11 | async-start | bytes 18874368 | tf_op jit(solution)/shard_map/psum | solution.py:137
  618.1 409.8 %reduce-scatter.9.cloned.1.call-start = ((), (), s32[]{:S(2)}) async-start(), calls=%async_computation.7 | async-start | bytes 2654208 | tf_op jit(solution)/shard_map/reduce_scatter | solution.py:193
  627.3 428.4 %reduce-scatter.11.cloned.1.call-start = ((), (), s32[]{:S(2)}) async-start(), calls=%async_computation.8 | async-start | bytes 2654208 | tf_op jit(solution)/shard_map/reduce_scatter | solution.py:194
  627.6 345.1 %copy-start.15 = (f32[3072]{0:T(1024)S(1)}, f32[3072]{0:T(1024)}, u32[]{:S(2)}) copy-start(f32[3072]{0:T(1024)} %copy-done.14) | copy-start | bytes 36868
  627.6 345.1 %copy-start.17 = (f32[3072]{0:T(1024)S(1)}, f32[3072]{0:T(1024)}, u32[]{:S(2)}) copy-start(f32[3072]{0:T(1024)} %copy-done.16) | copy-start | bytes 36868
  639.2 325.0 %copy-start.13 = (f32[3072]{0:T(1024)S(1)}, f32[3072]{0:T(1024)}, u32[]{:S(2)}) copy-start(f32[3072]{0:T(1024)} %copy-done.12) | copy-start | bytes 36868
  639.2 325.0 %copy-start.20 = (f32[768]{0:T(1024)S(1)}, f32[768]{0:T(1024)}, u32[]{:S(2)}) copy-start(f32[768]{0:T(1024)} %param.25) | copy-start | bytes 9220
  639.2 475.9 %all-reduce.11.cloned.1.call-start = ((), (), s32[]{:S(2)}) async-start(), calls=%async_computation.6 | async-start | bytes 1572864 | tf_op jit(solution)/shard_map/psum | solution.py:205
  964.2 18.9 %slice-start = ((s8[9437184]{0:T(1024)(128)(4,1)}), s8[4194304]{0:T(1024)(128)(4,1)S(1)}, s32[]{:S(2)}) async-start(s8[9437184]{0:T(1024)(128)(4,1)} %bitcast.353), calls=%async_computation.12 | async-start | bytes 8388608
  964.2 18.9 %slice-start.1 = ((s8[9437184]{0:T(1024)(128)(4,1)}), s8[4194304]{0:T(1024)(128)(4,1)S(1)}, s32[]{:S(2)}) async-start(s8[9437184]{0:T(1024)(128)(4,1)} %bitcast.353), calls=%async_computation.13 | async-start | bytes 8388608
  964.2 18.9 %slice-start.6 = ((s8[9437184]{0:T(1024)(128)(4,1)}), s8[4194304]{0:T(1024)(128)(4,1)S(1)}, s32[]{:S(2)}) async-start(s8[9437184]{0:T(1024)(128)(4,1)} %bitcast.357), calls=%async_computation.18 | async-start | bytes 8388608
  964.2 18.9 %slice-start.7 = ((s8[9437184]{0:T(1024)(128)(4,1)}), s8[4194304]{0:T(1024)(128)(4,1)S(1)}, s32[]{:S(2)}) async-start(s8[9437184]{0:T(1024)(128)(4,1)} %bitcast.357), calls=%async_computation.19 | async-start | bytes 8388608
  964.2 18.9 %slice-start.9 = ((s8[4718592]{0:T(1024)(128)(4,1)}), s8[4194304]{0:T(1024)(128)(4,1)S(1)}, s32[]{:S(2)}) async-start(s8[4718592]{0:T(1024)(128)(4,1)} %bitcast.359), calls=%async_computation.21 | async-start | bytes 8388608
  972.7 10.4 slice-start.2
  972.7 10.4 slice-start.8
  972.7 10.4 slice-start.10
  994.8 8.7 copy-start.21
  994.8 8.7 copy-start.22
  994.8 8.7 copy-start.23
  994.8 8.7 copy-start.24
  994.8 8.7 copy-start.29
  994.8 122.4 %copy-start.1 = (bf16[1000,768]{1,0:T(8,128)(2,1)S(1)}, bf16[1000,768]{1,0:T(8,128)(2,1)}, u32[]{:S(2)}) copy-start(bf16[1000,768]{1,0:T(8,128)(2,1)} %param.24) | copy-start | bytes 4608004
  (15 other events, 52.0 us)
Sparse Core Ops, SparseCore 0:
  90.1 174.6 all-reduce.6
  309.2 170.9 all-reduce.8
  509.6 33.9 reduce-scatter.14
  597.3 39.1 reduce-scatter.12
  639.5 324.6 all-reduce.12
  968.0 41.3 reduce-scatter.8
  1013.2 42.3 reduce-scatter.10
  1059.4 55.6 all-reduce.10
where the time goes:
time: 1130 us; the launch traced here: 1120 us
  waiting for transfers between devices  690 us (61%)
  matrix products  141 us (12%)
  other arithmetic  139 us (12%)
  local copies, waits for them, and re-layouts  114 us (10%)
  blocking collectives  24.4 us (2%)
  between operations  15.4 us (1%)
    psum x1, waiting for transfers between devices, local(): lax.psum(mlp_part.astype(jnp.bfloat16), 'mp').astype(jnp.float32)  321 us
    psum x1, waiting for transfers between devices, local(): lax.psum(attn_part.astype(jnp.bfloat16), 'mp').astype(jnp.float32)  143 us
    psum x1, waiting for transfers between devices, local(): lax.psum(norm_part.astype(jnp.bfloat16), 'mp').astype(jnp.float32)  138 us
    psum x1, waiting for transfers between devices, local(): lax.psum((table_grad, grad_gain_one, grad_shift_one, grad_out_bias, grad_...  59.4 us
    reduce_sum x4, other arithmetic, layer_norm(): return offset * lax.rsqrt(spread + 1e-05) * gain_vec + shift_vec  35.5 us
    reduce_scatter x1, waiting for transfers between devices, local(): lax.psum_scatter(grad_down, 'dp', scatter_dimension=1, tiled=True)  27.8 us
    psum x1, blocking collectives, local(): lax.psum((table_grad, grad_gain_one, grad_shift_one, grad_out_bias, grad_...  24.4 us
    reduce_sum x3, other arithmetic, layer_norm(): centre = jnp.mean(rows_in, axis=-1, keepdims=True)  23.9 us
  transfers between devices with their start and end apart: 8, of which 5 were waited for; matrix products, arithmetic and copies ran while one was open for 21% of the time, Pallas kernels for 0%

commit v1 on v0

--- a/solution.py
+++ b/solution.py
@@ -3,6 +3,7 @@
 import jax.numpy as jnp
 from jax import lax
 from jax.sharding import PartitionSpec as P
+from jax.lax import all_gather
 
 HD = 64
 LEN_A = 128
@@ -94,6 +95,10 @@
     down_weight,
     down_bias,
 ):
+
+    def scan_rates_in(sheet, mesh_dim):
+        return jnp.sum(all_gather(sheet, mesh_dim), axis=0)
+
     count = hidden.shape[0]
     width = hidden.shape[1]
     local_width = qkv_weight.shape[2]
@@ -129,7 +134,7 @@
 
     normed, shaped, context, log_total = front(stream_in)
     attn_part = jnp.dot(context, out_weight, preferred_element_type=jnp.float32)
-    attn_total = lax.psum(attn_part.astype(jnp.bfloat16), "mp").astype(jnp.float32)
+    attn_total = scan_rates_in(attn_part.astype(jnp.bfloat16), "mp").astype(jnp.float32)
     middle = stream_in + attn_total + out_bias
     normed_two = layer_norm(middle, second_gain, second_shift).astype(jnp.bfloat16)
     pre_act, activated = mlp_front(normed_two)

time: 1130 us -> 1300 us (1.15)
  waiting for transfers between devices: 690 us -> 839 us
  other arithmetic: 139 us -> 154 us
    all_gather x0 -> x1, waiting for transfers between devices: none -> 292 us  [scan_rates_in(): return jnp.sum(all_gather(sheet, mesh_dim), axis=0)]
    psum x1 -> x0, waiting for transfers between devices: 143 us -> none  [local(): lax.psum(attn_part.astype(jnp.bfloat16), 'mp').astype(jnp.float32)]
    reduce_sum x0 -> x1, other arithmetic: none -> 13.6 us  [scan_rates_in(): return jnp.sum(all_gather(sheet, mesh_dim), axis=0)]
  transfers between devices with their start and end apart: 8 -> 8, of which waited for: 5 -> 5; matrix products, arithmetic and copies ran while one was open for 21% -> 18% of each run, Pallas kernels for 0% -> 0%
where the time goes in v1:
time: 1300 us; the launch traced here: 1290 us
  waiting for transfers between devices  839 us (65%)
  other arithmetic  154 us (12%)
  matrix products  141 us (11%)
  local copies, waits for them, and re-layouts  114 us (9%)
  blocking collectives  24.3 us (2%)
  between operations  15.4 us (1%)
    psum x1, waiting for transfers between devices, local(): lax.psum(mlp_part.astype(jnp.bfloat16), 'mp').astype(jnp.float32)  321 us
    all_gather x1, waiting for transfers between devices, scan_rates_in(): return jnp.sum(all_gather(sheet, mesh_dim), axis=0)  292 us
    psum x1, waiting for transfers between devices, local(): lax.psum(norm_part.astype(jnp.bfloat16), 'mp').astype(jnp.float32)  138 us
    psum x1, waiting for transfers between devices, local(): lax.psum((table_grad, grad_gain_one, grad_shift_one, grad_out_bias, grad_...  59.4 us
    reduce_sum x4, other arithmetic, layer_norm(): return offset * lax.rsqrt(spread + 1e-05) * gain_vec + shift_vec  35.6 us
    reduce_scatter x1, waiting for transfers between devices, local(): lax.psum_scatter(grad_down, 'dp', scatter_dimension=1, tiled=True)  27.8 us
  transfers between devices with their start and end apart: 8, of which 5 were waited for; matrix products, arithmetic and copies ran while one was open for 18% of the time, Pallas kernels for 0%

profile of v1, /device:TPU:0, one launch (start us, length us, event | category | flops | bytes accessed | tf_op | source)
XLA Modules:
  0.0 1288.6 jit_solution(6825914234867102181)
XLA Ops:
  12.4 6.6 pad_maximum_fusion
  19.0 9.8 fusion.139
  28.8 4.9 multiply_reduce_fusion.4
  35.2 3.5 fusion.104
  40.8 3.5 squeeze.178
  44.4 4.0 squeeze.177
  51.1 31.5 %while.45 = (s32[]{:T(128)}, bf16[3,2,512,3,64]{2,4,3,1,0:T(8,128)(2,1)}, bf16[3,2,512,3,64]{2,1,0,4,3:T(2,128)(2,1)}, bf16[3,2,512,3,64]{2,1,0,4,3:T(2,128)(2,1...) while((s32[]{:T(128)}, bf16[3,2,512,3,64]{2,4,3,1,0:T(8,128)(2,1)}, ...), condition=%wide.region_7.8_spmd, body=%wide.region_2.7_spmd.sunk | while | flops 421284864 | bytes 25809020 | solution.py:128
  86.5 3.6 convolution_convert_fusion.2
  90.3 4.2 reduce_sum.314
  94.5 4.8 multiply_reduce_fusion.2
  99.4 6.4 add_convert_fusion
  110.5 4.0 squeeze.181
  123.5 292.1 %all-gather.3.cloned.1.call-done = bf16[12288,768]{1,0:T(8,128)(2,1)} async-done(((bf16[3072,768]{1,0:T(8,128)(2,1)}), bf16[12288,768]{1,0:T(8,128)(2,1)}) %all-gather.3.cloned.1.call-update) | async-done | bytes 18874384 | tf_op jit(solution)/shard_map/all_gather | solution.py:100
  415.7 13.6 %reduce_sum.311 = bf16[3072,768]{1,0:T(8,128)(2,1)} reduce(bf16[4,3072,768]{2,1,0:T(8,128)(2,1)} %bitcast.362, bf16[]{:T(256)} %constant.349.clone.1), dimensions={0}, to_apply=%region_8.9 | reduce | flops 7077888 | bytes 23592962 | tf_op jit(solution)/shard_map/reduce_sum | solution.py:100
  429.2 10.0 fusion.138
  439.2 4.9 multiply_reduce_fusion.3
  447.3 6.4 fusion.143
  453.8 11.9 convert_reduce_fusion.3
  467.9 5.5 convolution_convert_fusion
  474.6 24.6 %while.46 = (s32[]{:T(128)}, bf16[3,2,512,3,64]{2,4,3,1,0:T(8,128)(2,1)}, f32[3,2,3,512]{3,2,1,0:T(4,128)S(1)}, bf16[3,2,512,3,64]{2,4,3,1,0:T(8,128)(2,1)}, bf1...) while((s32[]{:T(128)}, ...), condition=%wide.region_22.23_spmd, body=%wide.region_17.22_spmd.sunk | while | flops 421300224 | bytes 23522436 | solution.py:128
  499.2 3.5 copy.103
  502.7 3.9 convert_element_type.178
  506.6 137.7 %all-reduce.6.cloned.1.call-done = bf16[3072,768]{1,0:T(8,128)(2,1)} async-done(((bf16[3072,768]{1,0:T(8,128)(2,1)}), bf16[3072,768]{1,0:T(8,128)(2,1)}) %all-reduce.6.cloned.1.call-update) | async-done | bytes 4718608 | tf_op jit(solution)/shard_map/psum | solution.py:153
  644.4 8.4 convert_reduce_fusion.1
  652.8 8.3 fusion.102
  661.2 5.4 fusion.136
  666.6 3.3 convolution_convert_fusion.3
  673.7 4.4 reshape.677
  681.5 43.6 %while.47 = (s32[]{:T(128)}, bf16[3,2,512,3,64]{2,4,3,1,0:T(8,128)(2,1)}, bf16[3,2,512,3,64]{2,4,3,1,0:T(8,128)(2,1)}, bf16[3,2,512,3,64]{2,4,3,1,0:T(8,128)(2,1...) while((s32[]{:T(128)}, ...), condition=%wide.region_26.27_spmd, body=%wide.region_23.26_spmd.sunk | while | flops 1024463872 | bytes 55389380 | solution.py:165
  725.1 3.5 copy.102
  728.7 3.6 stack.128
  732.2 3.5 copy.100
  735.8 3.9 stack.126
  742.0 3.3 stack.127
  748.6 5.2 fusion.115
  756.5 4.8 reshape.698
  761.5 12.6 convolution_convert_fusion.1
  774.0 8.2 bitcast_convert_fusion
  782.3 9.1 fusion.144
  791.8 11.5 fusion.111
  807.0 321.4 %all-reduce.10.cloned.1.call-done = (bf16[3072,768]{1,0:T(8,128)(2,1)}, bf16[3072,768]{1,0:T(8,128)(2,1)}) async-done(((bf16[3072,768]{1,0:T(8,128)(2,1)}, bf16[3072,768]{1,0:T(8,128)(2,1)}), (bf16[3072,768]{1,0:T(8,128)(2,1)}, bf16[3072,768]{1,0:T(8,128)(2,1)})) %all-reduce.10.cloned.1.call-update) | async-done | bytes 9437200 | tf_op jit(solution)/shard_map/psum | solution.py:142
  1128.4 8.7 convert_reduce_fusion
  1137.2 10.2 fusion.103
  1147.4 6.6 fusion.137
  1159.1 8.6 add_convert_fusion.1
  1167.8 24.3 %all-reduce = (f32[768]{0:T(1024)}, f32[768]{0:T(1024)}, f32[768]{0:T(1024)}, f32[768]{0:T(1024)}, f32[768]{0:T(1024)}, /*index=5*/f32[768]{0:T(1024)}, f32[768]{0:T(1024)}) all-reduce(f32[768]{0:T(1024)S(1)} %get-tuple-element.458, f32[768]{0:T(1024)S(1)} %get-tuple-element.462, ...), channel_id=1, replica_groups=mesh['dp'=8,'mp'=4] {'dp'}, use_global_device_ids=true, to_apply=%region_34.35 | all-reduce | flops 5376 | bytes 43008 | tf_op jit(solution)/shard_map/psum | solution.py:210
  1192.1 27.8 %reduce-scatter.11.cloned.1.call-done = f32[768,96]{0,1:T(8,128)} async-done(((f32[768,768]{0,1:T(8,128)}), f32[768,96]{0,1:T(8,128)}) %reduce-scatter.11.cloned.1.call-update) | async-done | bytes 294928 | tf_op jit(solution)/shard_map/reduce_scatter | solution.py:199
  1219.8 59.4 %all-reduce.8.cloned.1.call-done = f32[1000,192]{0,1:T(8,128)} async-done(((f32[1000,192]{0,1:T(8,128)}), f32[1000,192]{0,1:T(8,128)}) %all-reduce.8.cloned.1.call-update) | async-done | bytes 768016 | tf_op jit(solution)/shard_map/psum | solution.py:210
  (351 shorter events, 161.3 us)
Async XLA Ops:
  7.2 408.5 %all-gather.3.cloned.1.call-start = ((), (), s32[]{:S(2)}) async-start(), calls=%async_computation.8 | async-start | bytes 23592960 | tf_op jit(solution)/shard_map/all_gather | solution.py:100
  19.0 14.8 %copy-start.35 = (bf16[3,768,192]{1,2,0:T(8,128)(2,1)S(1)}, bf16[3,768,192]{1,2,0:T(8,128)(2,1)}, u32[]{:S(2)}) copy-start(bf16[3,768,192]{1,2,0:T(8,128)(2,1)} %param.27) | copy-start | bytes 2654212
  28.8 5.0 copy-start.12
  28.8 6.4 copy-start.2
  28.8 6.4 copy-start.19
  28.8 6.4 copy-start.25
  90.2 554.2 %all-reduce.6.cloned.1.call-start = ((), (), s32[]{:S(2)}) async-start(), calls=%async_computation.4 | async-start | bytes 9437184 | tf_op jit(solution)/shard_map/psum | solution.py:153
  99.4 6.4 copy-start.36
  415.7 13.6 %copy-start.26 = (f32[768]{0:T(1024)S(1)}, f32[768]{0:T(1024)}, u32[]{:S(2)}) copy-start(f32[768]{0:T(1024)} %param.29) | copy-start | bytes 9220
  439.2 6.4 copy-start.3
  439.2 6.4 copy-start.18
  439.2 6.4 copy-start.27
  445.6 8.3 slice-start.11
  447.3 6.5 copy-start.7
  447.3 6.5 slice-start.12
  447.3 6.5 copy-start.33
  447.3 6.5 copy-start.37
  473.4 330.0 %reduce-scatter.15.cloned.1.call-start = ((), (), s32[]{:S(2)}) async-start(), calls=%async_computation.10 | async-start | bytes 884736
  644.4 8.4 copy-start.5
  644.4 16.8 %slice-start.3 = ((s8[9437184]{0:T(1024)(128)(4,1)}), s8[4194304]{0:T(1024)(128)(4,1)S(1)}, s32[]{:S(2)}) async-start(s8[9437184]{0:T(1024)(128)(4,1)} %bitcast.356), calls=%async_computation.15 | async-start | bytes 8388608
  644.4 16.8 %slice-start.4 = ((s8[9437184]{0:T(1024)(128)(4,1)}), s8[4194304]{0:T(1024)(128)(4,1)S(1)}, s32[]{:S(2)}) async-start(s8[9437184]{0:T(1024)(128)(4,1)} %bitcast.356), calls=%async_computation.16 | async-start | bytes 8388608
  644.4 16.8 %slice-start.13 = ((s8[4718592]{0:T(1024)(128)(4,1)}), s8[4194304]{0:T(1024)(128)(4,1)S(1)}, s32[]{:S(2)}) async-start(s8[4718592]{0:T(1024)(128)(4,1)} %bitcast.372), calls=%async_computation.25 | async-start | bytes 8388608
  652.8 8.4 slice-start.5
  652.8 8.4 slice-start.14
  673.6 131.4 %reduce-scatter.13.cloned.1.call-start = ((), (), s32[]{:S(2)}) async-start(), calls=%async_computation.9 | async-start | bytes 2211840
  728.7 11.0 copy-start.8
  761.4 367.0 %all-reduce.10.cloned.1.call-start = ((), (), s32[]{:S(2)}) async-start(), calls=%async_computation.11 | async-start | bytes 18874368 | tf_op jit(solution)/shard_map/psum | solution.py:142
  782.3 409.8 %reduce-scatter.9.cloned.1.call-start = ((), (), s32[]{:S(2)}) async-start(), calls=%async_computation.6 | async-start | bytes 2654208 | tf_op jit(solution)/shard_map/reduce_scatter | solution.py:198
  791.5 428.4 %reduce-scatter.11.cloned.1.call-start = ((), (), s32[]{:S(2)}) async-start(), calls=%async_computation.7 | async-start | bytes 2654208 | tf_op jit(solution)/shard_map/reduce_scatter | solution.py:199
  791.8 345.3 %copy-start.15 = (f32[3072]{0:T(1024)S(1)}, f32[3072]{0:T(1024)}, u32[]{:S(2)}) copy-start(f32[3072]{0:T(1024)} %copy-done.14) | copy-start | bytes 36868
  791.8 345.3 %copy-start.17 = (f32[3072]{0:T(1024)S(1)}, f32[3072]{0:T(1024)}, u32[]{:S(2)}) copy-start(f32[3072]{0:T(1024)} %copy-done.16) | copy-start | bytes 36868
  803.3 325.0 %copy-start.13 = (f32[3072]{0:T(1024)S(1)}, f32[3072]{0:T(1024)}, u32[]{:S(2)}) copy-start(f32[3072]{0:T(1024)} %copy-done.12) | copy-start | bytes 36868
  803.3 325.0 %copy-start.20 = (f32[768]{0:T(1024)S(1)}, f32[768]{0:T(1024)}, u32[]{:S(2)}) copy-start(f32[768]{0:T(1024)} %param.25) | copy-start | bytes 9220
  803.4 475.9 %all-reduce.8.cloned.1.call-start = ((), (), s32[]{:S(2)}) async-start(), calls=%async_computation.5 | async-start | bytes 1572864 | tf_op jit(solution)/shard_map/psum | solution.py:210
  1128.4 19.0 %slice-start = ((s8[9437184]{0:T(1024)(128)(4,1)}), s8[4194304]{0:T(1024)(128)(4,1)S(1)}, s32[]{:S(2)}) async-start(s8[9437184]{0:T(1024)(128)(4,1)} %bitcast.354), calls=%async_computation.12 | async-start | bytes 8388608
  1128.4 19.0 %slice-start.1 = ((s8[9437184]{0:T(1024)(128)(4,1)}), s8[4194304]{0:T(1024)(128)(4,1)S(1)}, s32[]{:S(2)}) async-start(s8[9437184]{0:T(1024)(128)(4,1)} %bitcast.354), calls=%async_computation.13 | async-start | bytes 8388608
  1128.4 19.0 %slice-start.6 = ((s8[9437184]{0:T(1024)(128)(4,1)}), s8[4194304]{0:T(1024)(128)(4,1)S(1)}, s32[]{:S(2)}) async-start(s8[9437184]{0:T(1024)(128)(4,1)} %bitcast.358), calls=%async_computation.18 | async-start | bytes 8388608
  1128.4 19.0 %slice-start.7 = ((s8[9437184]{0:T(1024)(128)(4,1)}), s8[4194304]{0:T(1024)(128)(4,1)S(1)}, s32[]{:S(2)}) async-start(s8[9437184]{0:T(1024)(128)(4,1)} %bitcast.358), calls=%async_computation.19 | async-start | bytes 8388608
  1128.4 19.0 %slice-start.9 = ((s8[4718592]{0:T(1024)(128)(4,1)}), s8[4194304]{0:T(1024)(128)(4,1)S(1)}, s32[]{:S(2)}) async-start(s8[4718592]{0:T(1024)(128)(4,1)} %bitcast.360), calls=%async_computation.21 | async-start | bytes 8388608
  1137.1 10.3 slice-start.2
  1137.1 10.3 slice-start.8
  1137.1 10.3 slice-start.10
  1159.0 8.7 copy-start.21
  1159.0 8.7 copy-start.22
  1159.0 8.7 copy-start.23
  1159.1 8.7 copy-start.24
  1159.1 8.7 copy-start.29
  1159.1 122.3 %copy-start.1 = (bf16[1000,768]{1,0:T(8,128)(2,1)S(1)}, bf16[1000,768]{1,0:T(8,128)(2,1)}, u32[]{:S(2)}) copy-start(bf16[1000,768]{1,0:T(8,128)(2,1)} %param.24) | copy-start | bytes 4608004
  (15 other events, 52.0 us)
Sparse Core Ops, SparseCore 0:
  90.3 325.2 all-gather.2
  473.5 170.7 all-reduce.5
  673.8 33.9 reduce-scatter.14
  761.5 39.0 reduce-scatter.12
  803.6 324.6 all-reduce.9
  1132.1 41.2 reduce-scatter.8
  1177.4 42.4 reduce-scatter.10
  1223.6 55.6 all-reduce.7
